TPU v7x, 32 devices: a whole 2x2x4 slice. The times are simulated.
32 devices in a mesh: section: 4 (over z), space: 8 (over y, x, core).
Axes of the slice: x: 2, y: 2, z: 4, core: 2. Of those that a mesh axis runs over, the one named last changes fastest.
Arguments:
- act_in: bfloat16 [4, 4096, 512], P('section', 'space'), may hold values from -6 to 6
- stash: bfloat16 [4, 4, 4096, 512], P('section', None, 'space'), may hold values from -6 to 6
- plan: int32 [4], P('section'), may hold values from 0 to 3
- grad_in: bfloat16 [4, 4096, 512], P('section', 'space'), may hold values from -6 to 6
- fwd_owner: int32 [4, 4096], P('section', 'space'), may hold values from 0 to 7, as said below
- stash_owner: int32 [4, 4, 4096], P('section', None, 'space'), may hold values from 0 to 7, as said below
- ln_gain: float32 [4, 512], P('section'), may hold values from 0.5 to 1.5
- qkv_weight: bfloat16 [4, 512, 1536], P('section')
- proj_weight: bfloat16 [4, 512, 512], P('section'), may hold values from -1 to 1
Outputs:
- act_out: bfloat16 [4, 4096, 512], P('section', 'space')
- grad_out: bfloat16 [4, 4096, 512], P('section', 'space')
Inputs may be any that keep to these rules, and one draw needn't show every extreme that they name: `fwd_owner`: within each group of 512 rows of one list, owners never decrease; each group sends 128 rows to a quarter of the owners, 64 rows to half of them and none to the rest; in each list one owner gets 128 rows from every group. `stash_owner`: same law for each section and stored microbatch, independently drawn.
All inputs are finite; a program needn't handle non-finite values.
Results may differ from a plain program's by a relative error of at most 0.004.
The roundings to bfloat16 on the way count: a program that leaves them out, or rounds other values in their place, can miss the bound.
Values may be sent and summed in bfloat16 or wider, within the bound.
A program may use at most 128 MiB of HBM per device.

v0:
```python
import math
import jax
import jax.numpy as jnp
from jax import lax
from jax.sharding import PartitionSpec as P

HEADS = 32
EPS = 1e-05
NEG = -1e30
HEAD_GROUP = 2


def passed_along(value, axis, by):
    size = lax.axis_size(axis)
    pairs = [(i, i + by) for i in range(size) if 0 <= i + by < size]
    return lax.ppermute(value, axis, pairs)


def normalize(rows_in, gain):
    values = rows_in.astype(jnp.float32)
    center = values - jnp.mean(values, axis=-1, keepdims=True)
    spread = jnp.mean(center * center, axis=-1, keepdims=True)
    return center * lax.rsqrt(spread + EPS) * gain


def split_heads(block, head_dim):
    return block.reshape(block.shape[0], block.shape[1] // head_dim, head_dim)


def block_probs(query, key_rows, live, scale):
    score = jnp.einsum("qhd,khd->hqk", query, key_rows, preferred_element_type=jnp.float32) * scale
    score = jnp.where(live[None, None, :], score, NEG)
    top = jnp.max(score, axis=2, keepdims=True)
    expd = jnp.exp(score - top)
    return expd / jnp.sum(expd, axis=2, keepdims=True)


def attend(patch, live, heads):
    width = patch.shape[1] // 3
    head_dim = width // heads
    span = HEAD_GROUP * head_dim
    scale = 1.0 / math.sqrt(head_dim)
    slots = patch.shape[0]

    def one_block(block_index, totals):
        start = block_index * span
        query = split_heads(lax.dynamic_slice_in_dim(patch, start, span, 1), head_dim)
        key_rows = split_heads(lax.dynamic_slice_in_dim(patch, width + start, span, 1), head_dim)
        value_rows = split_heads(
            lax.dynamic_slice_in_dim(patch, 2 * width + start, span, 1), head_dim
        )
        probs = block_probs(query, key_rows, live, scale).astype(jnp.bfloat16)
        result = jnp.einsum(
            "hqk,khd->qhd", probs, value_rows, preferred_element_type=jnp.float32
        ).reshape(slots, span)
        return lax.dynamic_update_slice_in_dim(totals, result, start, 1)

    return lax.fori_loop(0, heads // HEAD_GROUP, one_block, jnp.zeros((slots, width), jnp.float32))


def attend_grad(patch, live, upstream, heads):
    width = patch.shape[1] // 3
    head_dim = width // heads
    span = HEAD_GROUP * head_dim
    scale = 1.0 / math.sqrt(head_dim)
    slots = patch.shape[0]

    def one_block(block_index, totals):
        start = block_index * span
        query = split_heads(lax.dynamic_slice_in_dim(patch, start, span, 1), head_dim)
        key_rows = split_heads(lax.dynamic_slice_in_dim(patch, width + start, span, 1), head_dim)
        value_rows = split_heads(
            lax.dynamic_slice_in_dim(patch, 2 * width + start, span, 1), head_dim
        )
        out_grad = split_heads(lax.dynamic_slice_in_dim(upstream, start, span, 1), head_dim)
        probs = block_probs(query, key_rows, live, scale)
        rounded = probs.astype(jnp.bfloat16)
        prob_grad = jnp.einsum(
            "qhd,khd->hqk", out_grad, value_rows, preferred_element_type=jnp.float32
        )
        value_grad = jnp.einsum(
            "hqk,qhd->khd", rounded, out_grad, preferred_element_type=jnp.float32
        ).reshape(slots, span)
        delta = jnp.sum(prob_grad * probs, axis=2, keepdims=True)
        score_grad = (probs * (prob_grad - delta) * scale).astype(jnp.bfloat16)
        query_grad = jnp.einsum(
            "hqk,khd->qhd", score_grad, key_rows, preferred_element_type=jnp.float32
        ).reshape(slots, span)
        key_grad = jnp.einsum(
            "hqk,qhd->khd", score_grad, query, preferred_element_type=jnp.float32
        ).reshape(slots, span)
        totals = lax.dynamic_update_slice_in_dim(totals, query_grad, start, 1)
        totals = lax.dynamic_update_slice_in_dim(totals, key_grad, width + start, 1)
        return lax.dynamic_update_slice_in_dim(totals, value_grad, 2 * width + start, 1)

    return lax.fori_loop(
        0, heads // HEAD_GROUP, one_block, jnp.zeros((slots, 3 * width), jnp.float32)
    )


def layout(owners, groups, cap):
    rows = owners.shape[0]
    labels = jnp.arange(groups, dtype=jnp.int32)
    onehot = (owners[:, None] == labels[None, :]).astype(jnp.int32)
    counts = jnp.sum(onehot, axis=0)
    offsets = jnp.cumsum(counts) - counts
    slots = jnp.arange(cap, dtype=jnp.int32)
    valid = slots[None, :] < counts[:, None]
    index = jnp.where(valid, offsets[:, None] + slots[None, :], 0)
    rank = jnp.arange(rows, dtype=jnp.int32) - jnp.sum(onehot * offsets[None, :], axis=1)
    back = owners * cap + rank
    return (index, valid, back)


def pack_rows(source, index, valid):
    picked = jnp.take(source, index.reshape(-1), axis=0).reshape(index.shape + (source.shape[1],))
    return jnp.where(valid[..., None], picked, jnp.zeros((), source.dtype))


def project(rows_in, w_qkv):
    return jnp.dot(rows_in, w_qkv, preferred_element_type=jnp.float32).astype(jnp.bfloat16)


def on_device(
    act_in, stash, plan, grad_in, fwd_owner, stash_owner, ln_gain, qkv_weight, proj_weight
):
    groups = lax.axis_size("space")
    rows_in = act_in[0]
    rows = rows_in.shape[0]
    width = rows_in.shape[1]
    cap = 2 * rows // groups
    slots_all = groups * cap
    gain = ln_gain[0]
    w_qkv = qkv_weight[0]
    w_proj = proj_weight[0]
    pick = plan[0]
    stored = lax.dynamic_index_in_dim(stash[0], pick, 0, keepdims=False)
    stored_owners = lax.dynamic_index_in_dim(stash_owner[0], pick, 0, keepdims=False)
    upstream = grad_in[0]
    normed = normalize(rows_in, gain).astype(jnp.bfloat16)
    normed_b = normalize(stored, gain).astype(jnp.bfloat16)
    out_grad = jnp.dot(upstream, w_proj.T, preferred_element_type=jnp.float32).astype(jnp.bfloat16)
    payload = project(normed, w_qkv)
    payload_b = project(normed_b, w_qkv)
    index, valid, back = layout(fwd_owner[0], groups, cap)
    index_b, valid_b, back_b = layout(stored_owners, groups, cap)
    send_rows = pack_rows(payload, index, valid)
    send_flags = valid.astype(jnp.bfloat16)
    send_rows_b = pack_rows(payload_b, index_b, valid_b)
    send_flags_b = valid_b.astype(jnp.bfloat16)
    send_grads = pack_rows(out_grad, index_b, valid_b)
    got_rows, got_flags = (
        lax.all_to_all(send_rows, "space", split_axis=0, concat_axis=0, tiled=True),
        lax.all_to_all(send_flags, "space", split_axis=0, concat_axis=0, tiled=True),
    )
    got_rows_b, got_flags_b = (
        lax.all_to_all(send_rows_b, "space", split_axis=0, concat_axis=0, tiled=True),
        lax.all_to_all(send_flags_b, "space", split_axis=0, concat_axis=0, tiled=True),
    )
    got_grads = lax.all_to_all(send_grads, "space", split_axis=0, concat_axis=0, tiled=True)
    patch = got_rows.reshape(slots_all, got_rows.shape[-1])
    patch_b = got_rows_b.reshape(slots_all, got_rows_b.shape[-1])
    live = got_flags.reshape(slots_all) > 0.5
    live_b = got_flags_b.reshape(slots_all) > 0.5
    attended = attend(patch, live, HEADS).astype(jnp.bfloat16).reshape(groups, cap, width)
    qkv_grads = attend_grad(patch_b, live_b, got_grads.reshape(slots_all, width), HEADS).astype(
        jnp.bfloat16
    )
    slot_qkv = qkv_grads.reshape(groups, cap, 3 * width)
    ret_att = lax.all_to_all(attended, "space", split_axis=0, concat_axis=0, tiled=True)
    ret_grads = lax.all_to_all(slot_qkv, "space", split_axis=0, concat_axis=0, tiled=True)
    grad_rows = jnp.take(ret_grads.reshape(slots_all, 3 * width), back_b, axis=0)
    normed_grad = jnp.dot(grad_rows, w_qkv.T, preferred_element_type=jnp.float32)
    att_rows = jnp.take(ret_att.reshape(slots_all, width), back, axis=0)
    mixed = (
        rows_in.astype(jnp.float32) + jnp.dot(att_rows, w_proj, preferred_element_type=jnp.float32)
    ).astype(jnp.bfloat16)
    unused, pull = jax.vjp(lambda values: normalize(values, gain), stored.astype(jnp.float32))
    input_grad = (upstream.astype(jnp.float32) + pull(normed_grad)[0]).astype(jnp.bfloat16)
    act_out = passed_along(mixed[None], "section", 1)
    grad_out = passed_along(input_grad[None], "section", -1)
    return (act_out, grad_out)


def solution(mesh):
    in_specs = (
        P("section", "space", None),
        P("section", None, "space", None),
        P("section"),
        P("section", "space", None),
        P("section", "space"),
        P("section", None, "space"),
        P("section", None),
        P("section", None, None),
        P("section", None, None),
    )
    out_specs = (P("section", "space", None), P("section", "space", None))
    return jax.shard_map(
        on_device, mesh=mesh, in_specs=in_specs, out_specs=out_specs, check_vma=False
    )
```

profile of v0, /device:TPU:18, one launch (start us, length us, event | category | flops | bytes accessed | tf_op | source)
XLA Modules:
  0.0 1101.2 jit_solution(14951067177431255770)
XLA Ops:
  44.7 9.5 all-to-all-done.5
  72.7 23.9 %all-to-all-done.3 = bf16[8,128,1536]{2,1,0:T(8,128)(2,1)} async-done(((bf16[8,128,1536]{2,1,0:T(8,128)(2,1)}), bf16[8,128,1536]{2,1,0:T(8,128)(2,1)}, u32[]{:S(2)}, u32[]{:S(2)}) %all-to-all-start.3) | async-done | bytes 3145760 | tf_op jit(solution)/shard_map/all_to_all | solution.py:157
  107.6 31.3 %all-to-all-done = bf16[8,128,1536]{2,1,0:T(8,128)(2,1)} async-done(((bf16[8,128,1536]{2,1,0:T(8,128)(2,1)}), bf16[8,128,1536]{2,1,0:T(8,128)(2,1)}, u32[]{:S(2)}, u32[]{:S(2)}) %all-to-all-start) | async-done | bytes 3145760 | tf_op jit(solution)/shard_map/all_to_all | solution.py:153
  143.7 179.0 %while.30 = (s32[]{:T(128)}, bf16[1024,512]{0,1:T(8,128)(2,1)S(1)}, bf16[1024,1536]{0,1:T(8,128)(2,1)}, pred[1024]{0:T(1024)(128)(4,1)S(1)}, s32[]{:T(128)}, /*i...) while((s32[]{:T(128)}, bf16[1024,512]{0,1:T(8,128)(2,1)S(1)}, ...), condition=%wide.region_8.10_spmd, body=%wide.region_5.9_spmd.sunk | while | flops 146801680 | bytes 17581340 | solution.py:58
  144.7 6.2 fusion.130
  155.9 6.2 fusion.130
  167.1 6.2 fusion.130
  178.2 6.2 fusion.130
  189.4 6.2 fusion.130
  200.6 6.2 fusion.130
  211.8 6.2 fusion.130
  223.0 6.2 fusion.130
  245.4 6.2 fusion.130
  256.6 6.2 fusion.130
  267.8 6.2 fusion.130
  278.9 6.2 fusion.130
  290.1 6.2 fusion.130
  301.3 6.2 fusion.130
  312.5 6.2 fusion.130
  331.8 695.5 %while.31 = (s32[]{:T(128)}, bf16[1024,1536]{0,1:T(8,128)(2,1)}, bf16[1024,1536]{0,1:T(8,128)(2,1)}, pred[1024]{0:T(1024)(128)(4,1)S(1)}, bf16[1024,512]{0,1:T(8...) while((s32[]{:T(128)}, bf16[1024,1536]{0,1:T(8,128)(2,1)}, ...), condition=%wide.region_18.20_spmd, body=%wide.region_14.19_spmd.sunk | while | flops 377494528 | bytes 60327216 | solution.py:96
  332.7 6.2 fusion.143
  343.4 12.1 %fusion.145 = bf16[2,16,1024]{2,1,0:T(8,128)(2,1)S(1)} fusion(bf16[1024,2,16]{0,2,1:T(8,128)(2,1)S(1)} %bitcast.217, f32[2,1024,1024]{1,2,0:T(8,128)} %fusion.142, f32[2,1024,1024]{1,2,0:T(8,128)} %get-tuple-element.366, f32[2,1024]{1,0:T(2,128)S(1)} %get-tuple-element.367), kind=kOutput, calls=%fused_computation.35.clone.1 | convolution fusion | flops 81792000 | bytes 16916480 | tf_op jit(solution)/shard_map/while/body/eval_jaxpr/hqk,qhd->khd/dot_general | solution.py:89
  355.5 13.3 %fusion.144 = bf16[2,16,1024]{2,1,0:T(8,128)(2,1)S(1)} fusion(bf16[1024,2,16]{0,2,1:T(8,128)(2,1)S(1)} %bitcast.215, f32[2,1024,1024]{1,2,0:T(8,128)} %fusion.142, f32[2,1024,1024]{1,2,0:T(8,128)} %get-tuple-element.366, f32[2,1024]{1,0:T(2,128)S(1)} %get-tuple-element.367), kind=kOutput, calls=%fused_computation.36.clone.1 | convolution fusion | flops 81792000 | bytes 16916480 | tf_op jit(solution)/shard_map/while/body/eval_jaxpr/hqk,khd->qhd/dot_general | solution.py:86
  376.2 6.2 fusion.143
  386.9 12.1 %fusion.145 = bf16[2,16,1024]{2,1,0:T(8,128)(2,1)S(1)} fusion(bf16[1024,2,16]{0,2,1:T(8,128)(2,1)S(1)} %bitcast.217, f32[2,1024,1024]{1,2,0:T(8,128)} %fusion.142, f32[2,1024,1024]{1,2,0:T(8,128)} %get-tuple-element.366, f32[2,1024]{1,0:T(2,128)S(1)} %get-tuple-element.367), kind=kOutput, calls=%fused_computation.35.clone.1 | convolution fusion | flops 81792000 | bytes 16916480 | tf_op jit(solution)/shard_map/while/body/eval_jaxpr/hqk,qhd->khd/dot_general | solution.py:89
  399.0 13.3 %fusion.144 = bf16[2,16,1024]{2,1,0:T(8,128)(2,1)S(1)} fusion(bf16[1024,2,16]{0,2,1:T(8,128)(2,1)S(1)} %bitcast.215, f32[2,1024,1024]{1,2,0:T(8,128)} %fusion.142, f32[2,1024,1024]{1,2,0:T(8,128)} %get-tuple-element.366, f32[2,1024]{1,0:T(2,128)S(1)} %get-tuple-element.367), kind=kOutput, calls=%fused_computation.36.clone.1 | convolution fusion | flops 81792000 | bytes 16916480 | tf_op jit(solution)/shard_map/while/body/eval_jaxpr/hqk,khd->qhd/dot_general | solution.py:86
  419.7 6.2 fusion.143
  430.3 12.1 %fusion.145 = bf16[2,16,1024]{2,1,0:T(8,128)(2,1)S(1)} fusion(bf16[1024,2,16]{0,2,1:T(8,128)(2,1)S(1)} %bitcast.217, f32[2,1024,1024]{1,2,0:T(8,128)} %fusion.142, f32[2,1024,1024]{1,2,0:T(8,128)} %get-tuple-element.366, f32[2,1024]{1,0:T(2,128)S(1)} %get-tuple-element.367), kind=kOutput, calls=%fused_computation.35.clone.1 | convolution fusion | flops 81792000 | bytes 16916480 | tf_op jit(solution)/shard_map/while/body/eval_jaxpr/hqk,qhd->khd/dot_general | solution.py:89
  442.5 13.3 %fusion.144 = bf16[2,16,1024]{2,1,0:T(8,128)(2,1)S(1)} fusion(bf16[1024,2,16]{0,2,1:T(8,128)(2,1)S(1)} %bitcast.215, f32[2,1024,1024]{1,2,0:T(8,128)} %fusion.142, f32[2,1024,1024]{1,2,0:T(8,128)} %get-tuple-element.366, f32[2,1024]{1,0:T(2,128)S(1)} %get-tuple-element.367), kind=kOutput, calls=%fused_computation.36.clone.1 | convolution fusion | flops 81792000 | bytes 16916480 | tf_op jit(solution)/shard_map/while/body/eval_jaxpr/hqk,khd->qhd/dot_general | solution.py:86
  463.2 6.2 fusion.143
  473.8 12.1 %fusion.145 = bf16[2,16,1024]{2,1,0:T(8,128)(2,1)S(1)} fusion(bf16[1024,2,16]{0,2,1:T(8,128)(2,1)S(1)} %bitcast.217, f32[2,1024,1024]{1,2,0:T(8,128)} %fusion.142, f32[2,1024,1024]{1,2,0:T(8,128)} %get-tuple-element.366, f32[2,1024]{1,0:T(2,128)S(1)} %get-tuple-element.367), kind=kOutput, calls=%fused_computation.35.clone.1 | convolution fusion | flops 81792000 | bytes 16916480 | tf_op jit(solution)/shard_map/while/body/eval_jaxpr/hqk,qhd->khd/dot_general | solution.py:89
  485.9 13.3 %fusion.144 = bf16[2,16,1024]{2,1,0:T(8,128)(2,1)S(1)} fusion(bf16[1024,2,16]{0,2,1:T(8,128)(2,1)S(1)} %bitcast.215, f32[2,1024,1024]{1,2,0:T(8,128)} %fusion.142, f32[2,1024,1024]{1,2,0:T(8,128)} %get-tuple-element.366, f32[2,1024]{1,0:T(2,128)S(1)} %get-tuple-element.367), kind=kOutput, calls=%fused_computation.36.clone.1 | convolution fusion | flops 81792000 | bytes 16916480 | tf_op jit(solution)/shard_map/while/body/eval_jaxpr/hqk,khd->qhd/dot_general | solution.py:86
  517.3 12.1 %fusion.145 = bf16[2,16,1024]{2,1,0:T(8,128)(2,1)S(1)} fusion(bf16[1024,2,16]{0,2,1:T(8,128)(2,1)S(1)} %bitcast.217, f32[2,1024,1024]{1,2,0:T(8,128)} %fusion.142, f32[2,1024,1024]{1,2,0:T(8,128)} %get-tuple-element.366, f32[2,1024]{1,0:T(2,128)S(1)} %get-tuple-element.367), kind=kOutput, calls=%fused_computation.35.clone.1 | convolution fusion | flops 81792000 | bytes 16916480 | tf_op jit(solution)/shard_map/while/body/eval_jaxpr/hqk,qhd->khd/dot_general | solution.py:89
  529.4 13.3 %fusion.144 = bf16[2,16,1024]{2,1,0:T(8,128)(2,1)S(1)} fusion(bf16[1024,2,16]{0,2,1:T(8,128)(2,1)S(1)} %bitcast.215, f32[2,1024,1024]{1,2,0:T(8,128)} %fusion.142, f32[2,1024,1024]{1,2,0:T(8,128)} %get-tuple-element.366, f32[2,1024]{1,0:T(2,128)S(1)} %get-tuple-element.367), kind=kOutput, calls=%fused_computation.36.clone.1 | convolution fusion | flops 81792000 | bytes 16916480 | tf_op jit(solution)/shard_map/while/body/eval_jaxpr/hqk,khd->qhd/dot_general | solution.py:86
  550.1 6.2 fusion.143
  560.8 12.1 %fusion.145 = bf16[2,16,1024]{2,1,0:T(8,128)(2,1)S(1)} fusion(bf16[1024,2,16]{0,2,1:T(8,128)(2,1)S(1)} %bitcast.217, f32[2,1024,1024]{1,2,0:T(8,128)} %fusion.142, f32[2,1024,1024]{1,2,0:T(8,128)} %get-tuple-element.366, f32[2,1024]{1,0:T(2,128)S(1)} %get-tuple-element.367), kind=kOutput, calls=%fused_computation.35.clone.1 | convolution fusion | flops 81792000 | bytes 16916480 | tf_op jit(solution)/shard_map/while/body/eval_jaxpr/hqk,qhd->khd/dot_general | solution.py:89
  572.9 13.3 %fusion.144 = bf16[2,16,1024]{2,1,0:T(8,128)(2,1)S(1)} fusion(bf16[1024,2,16]{0,2,1:T(8,128)(2,1)S(1)} %bitcast.215, f32[2,1024,1024]{1,2,0:T(8,128)} %fusion.142, f32[2,1024,1024]{1,2,0:T(8,128)} %get-tuple-element.366, f32[2,1024]{1,0:T(2,128)S(1)} %get-tuple-element.367), kind=kOutput, calls=%fused_computation.36.clone.1 | convolution fusion | flops 81792000 | bytes 16916480 | tf_op jit(solution)/shard_map/while/body/eval_jaxpr/hqk,khd->qhd/dot_general | solution.py:86
  604.2 12.1 %fusion.145 = bf16[2,16,1024]{2,1,0:T(8,128)(2,1)S(1)} fusion(bf16[1024,2,16]{0,2,1:T(8,128)(2,1)S(1)} %bitcast.217, f32[2,1024,1024]{1,2,0:T(8,128)} %fusion.142, f32[2,1024,1024]{1,2,0:T(8,128)} %get-tuple-element.366, f32[2,1024]{1,0:T(2,128)S(1)} %get-tuple-element.367), kind=kOutput, calls=%fused_computation.35.clone.1 | convolution fusion | flops 81792000 | bytes 16916480 | tf_op jit(solution)/shard_map/while/body/eval_jaxpr/hqk,qhd->khd/dot_general | solution.py:89
  616.3 13.3 %fusion.144 = bf16[2,16,1024]{2,1,0:T(8,128)(2,1)S(1)} fusion(bf16[1024,2,16]{0,2,1:T(8,128)(2,1)S(1)} %bitcast.215, f32[2,1024,1024]{1,2,0:T(8,128)} %fusion.142, f32[2,1024,1024]{1,2,0:T(8,128)} %get-tuple-element.366, f32[2,1024]{1,0:T(2,128)S(1)} %get-tuple-element.367), kind=kOutput, calls=%fused_computation.36.clone.1 | convolution fusion | flops 81792000 | bytes 16916480 | tf_op jit(solution)/shard_map/while/body/eval_jaxpr/hqk,khd->qhd/dot_general | solution.py:86
  637.0 6.2 fusion.143
  647.7 12.1 %fusion.145 = bf16[2,16,1024]{2,1,0:T(8,128)(2,1)S(1)} fusion(bf16[1024,2,16]{0,2,1:T(8,128)(2,1)S(1)} %bitcast.217, f32[2,1024,1024]{1,2,0:T(8,128)} %fusion.142, f32[2,1024,1024]{1,2,0:T(8,128)} %get-tuple-element.366, f32[2,1024]{1,0:T(2,128)S(1)} %get-tuple-element.367), kind=kOutput, calls=%fused_computation.35.clone.1 | convolution fusion | flops 81792000 | bytes 16916480 | tf_op jit(solution)/shard_map/while/body/eval_jaxpr/hqk,qhd->khd/dot_general | solution.py:89
  659.8 13.3 %fusion.144 = bf16[2,16,1024]{2,1,0:T(8,128)(2,1)S(1)} fusion(bf16[1024,2,16]{0,2,1:T(8,128)(2,1)S(1)} %bitcast.215, f32[2,1024,1024]{1,2,0:T(8,128)} %fusion.142, f32[2,1024,1024]{1,2,0:T(8,128)} %get-tuple-element.366, f32[2,1024]{1,0:T(2,128)S(1)} %get-tuple-element.367), kind=kOutput, calls=%fused_computation.36.clone.1 | convolution fusion | flops 81792000 | bytes 16916480 | tf_op jit(solution)/shard_map/while/body/eval_jaxpr/hqk,khd->qhd/dot_general | solution.py:86
  680.5 6.2 fusion.143
  691.2 12.1 %fusion.145 = bf16[2,16,1024]{2,1,0:T(8,128)(2,1)S(1)} fusion(bf16[1024,2,16]{0,2,1:T(8,128)(2,1)S(1)} %bitcast.217, f32[2,1024,1024]{1,2,0:T(8,128)} %fusion.142, f32[2,1024,1024]{1,2,0:T(8,128)} %get-tuple-element.366, f32[2,1024]{1,0:T(2,128)S(1)} %get-tuple-element.367), kind=kOutput, calls=%fused_computation.35.clone.1 | convolution fusion | flops 81792000 | bytes 16916480 | tf_op jit(solution)/shard_map/while/body/eval_jaxpr/hqk,qhd->khd/dot_general | solution.py:89
  703.3 13.3 %fusion.144 = bf16[2,16,1024]{2,1,0:T(8,128)(2,1)S(1)} fusion(bf16[1024,2,16]{0,2,1:T(8,128)(2,1)S(1)} %bitcast.215, f32[2,1024,1024]{1,2,0:T(8,128)} %fusion.142, f32[2,1024,1024]{1,2,0:T(8,128)} %get-tuple-element.366, f32[2,1024]{1,0:T(2,128)S(1)} %get-tuple-element.367), kind=kOutput, calls=%fused_computation.36.clone.1 | convolution fusion | flops 81792000 | bytes 16916480 | tf_op jit(solution)/shard_map/while/body/eval_jaxpr/hqk,khd->qhd/dot_general | solution.py:86
  724.0 6.2 fusion.143
  734.6 12.1 %fusion.145 = bf16[2,16,1024]{2,1,0:T(8,128)(2,1)S(1)} fusion(bf16[1024,2,16]{0,2,1:T(8,128)(2,1)S(1)} %bitcast.217, f32[2,1024,1024]{1,2,0:T(8,128)} %fusion.142, f32[2,1024,1024]{1,2,0:T(8,128)} %get-tuple-element.366, f32[2,1024]{1,0:T(2,128)S(1)} %get-tuple-element.367), kind=kOutput, calls=%fused_computation.35.clone.1 | convolution fusion | flops 81792000 | bytes 16916480 | tf_op jit(solution)/shard_map/while/body/eval_jaxpr/hqk,qhd->khd/dot_general | solution.py:89
  746.7 13.3 %fusion.144 = bf16[2,16,1024]{2,1,0:T(8,128)(2,1)S(1)} fusion(bf16[1024,2,16]{0,2,1:T(8,128)(2,1)S(1)} %bitcast.215, f32[2,1024,1024]{1,2,0:T(8,128)} %fusion.142, f32[2,1024,1024]{1,2,0:T(8,128)} %get-tuple-element.366, f32[2,1024]{1,0:T(2,128)S(1)} %get-tuple-element.367), kind=kOutput, calls=%fused_computation.36.clone.1 | convolution fusion | flops 81792000 | bytes 16916480 | tf_op jit(solution)/shard_map/while/body/eval_jaxpr/hqk,khd->qhd/dot_general | solution.py:86
  778.1 12.1 %fusion.145 = bf16[2,16,1024]{2,1,0:T(8,128)(2,1)S(1)} fusion(bf16[1024,2,16]{0,2,1:T(8,128)(2,1)S(1)} %bitcast.217, f32[2,1024,1024]{1,2,0:T(8,128)} %fusion.142, f32[2,1024,1024]{1,2,0:T(8,128)} %get-tuple-element.366, f32[2,1024]{1,0:T(2,128)S(1)} %get-tuple-element.367), kind=kOutput, calls=%fused_computation.35.clone.1 | convolution fusion | flops 81792000 | bytes 16916480 | tf_op jit(solution)/shard_map/while/body/eval_jaxpr/hqk,qhd->khd/dot_general | solution.py:89
  790.2 13.3 %fusion.144 = bf16[2,16,1024]{2,1,0:T(8,128)(2,1)S(1)} fusion(bf16[1024,2,16]{0,2,1:T(8,128)(2,1)S(1)} %bitcast.215, f32[2,1024,1024]{1,2,0:T(8,128)} %fusion.142, f32[2,1024,1024]{1,2,0:T(8,128)} %get-tuple-element.366, f32[2,1024]{1,0:T(2,128)S(1)} %get-tuple-element.367), kind=kOutput, calls=%fused_computation.36.clone.1 | convolution fusion | flops 81792000 | bytes 16916480 | tf_op jit(solution)/shard_map/while/body/eval_jaxpr/hqk,khd->qhd/dot_general | solution.py:86
  810.9 6.2 fusion.143
  821.6 12.1 %fusion.145 = bf16[2,16,1024]{2,1,0:T(8,128)(2,1)S(1)} fusion(bf16[1024,2,16]{0,2,1:T(8,128)(2,1)S(1)} %bitcast.217, f32[2,1024,1024]{1,2,0:T(8,128)} %fusion.142, f32[2,1024,1024]{1,2,0:T(8,128)} %get-tuple-element.366, f32[2,1024]{1,0:T(2,128)S(1)} %get-tuple-element.367), kind=kOutput, calls=%fused_computation.35.clone.1 | convolution fusion | flops 81792000 | bytes 16916480 | tf_op jit(solution)/shard_map/while/body/eval_jaxpr/hqk,qhd->khd/dot_general | solution.py:89
  833.7 13.3 %fusion.144 = bf16[2,16,1024]{2,1,0:T(8,128)(2,1)S(1)} fusion(bf16[1024,2,16]{0,2,1:T(8,128)(2,1)S(1)} %bitcast.215, f32[2,1024,1024]{1,2,0:T(8,128)} %fusion.142, f32[2,1024,1024]{1,2,0:T(8,128)} %get-tuple-element.366, f32[2,1024]{1,0:T(2,128)S(1)} %get-tuple-element.367), kind=kOutput, calls=%fused_computation.36.clone.1 | convolution fusion | flops 81792000 | bytes 16916480 | tf_op jit(solution)/shard_map/while/body/eval_jaxpr/hqk,khd->qhd/dot_general | solution.py:86
  865.0 12.1 %fusion.145 = bf16[2,16,1024]{2,1,0:T(8,128)(2,1)S(1)} fusion(bf16[1024,2,16]{0,2,1:T(8,128)(2,1)S(1)} %bitcast.217, f32[2,1024,1024]{1,2,0:T(8,128)} %fusion.142, f32[2,1024,1024]{1,2,0:T(8,128)} %get-tuple-element.366, f32[2,1024]{1,0:T(2,128)S(1)} %get-tuple-element.367), kind=kOutput, calls=%fused_computation.35.clone.1 | convolution fusion | flops 81792000 | bytes 16916480 | tf_op jit(solution)/shard_map/while/body/eval_jaxpr/hqk,qhd->khd/dot_general | solution.py:89
  877.1 13.3 %fusion.144 = bf16[2,16,1024]{2,1,0:T(8,128)(2,1)S(1)} fusion(bf16[1024,2,16]{0,2,1:T(8,128)(2,1)S(1)} %bitcast.215, f32[2,1024,1024]{1,2,0:T(8,128)} %fusion.142, f32[2,1024,1024]{1,2,0:T(8,128)} %get-tuple-element.366, f32[2,1024]{1,0:T(2,128)S(1)} %get-tuple-element.367), kind=kOutput, calls=%fused_computation.36.clone.1 | convolution fusion | flops 81792000 | bytes 16916480 | tf_op jit(solution)/shard_map/while/body/eval_jaxpr/hqk,khd->qhd/dot_general | solution.py:86
  908.5 12.1 %fusion.145 = bf16[2,16,1024]{2,1,0:T(8,128)(2,1)S(1)} fusion(bf16[1024,2,16]{0,2,1:T(8,128)(2,1)S(1)} %bitcast.217, f32[2,1024,1024]{1,2,0:T(8,128)} %fusion.142, f32[2,1024,1024]{1,2,0:T(8,128)} %get-tuple-element.366, f32[2,1024]{1,0:T(2,128)S(1)} %get-tuple-element.367), kind=kOutput, calls=%fused_computation.35.clone.1 | convolution fusion | flops 81792000 | bytes 16916480 | tf_op jit(solution)/shard_map/while/body/eval_jaxpr/hqk,qhd->khd/dot_general | solution.py:89
  920.6 13.3 %fusion.144 = bf16[2,16,1024]{2,1,0:T(8,128)(2,1)S(1)} fusion(bf16[1024,2,16]{0,2,1:T(8,128)(2,1)S(1)} %bitcast.215, f32[2,1024,1024]{1,2,0:T(8,128)} %fusion.142, f32[2,1024,1024]{1,2,0:T(8,128)} %get-tuple-element.366, f32[2,1024]{1,0:T(2,128)S(1)} %get-tuple-element.367), kind=kOutput, calls=%fused_computation.36.clone.1 | convolution fusion | flops 81792000 | bytes 16916480 | tf_op jit(solution)/shard_map/while/body/eval_jaxpr/hqk,khd->qhd/dot_general | solution.py:86
  952.0 12.1 %fusion.145 = bf16[2,16,1024]{2,1,0:T(8,128)(2,1)S(1)} fusion(bf16[1024,2,16]{0,2,1:T(8,128)(2,1)S(1)} %bitcast.217, f32[2,1024,1024]{1,2,0:T(8,128)} %fusion.142, f32[2,1024,1024]{1,2,0:T(8,128)} %get-tuple-element.366, f32[2,1024]{1,0:T(2,128)S(1)} %get-tuple-element.367), kind=kOutput, calls=%fused_computation.35.clone.1 | convolution fusion | flops 81792000 | bytes 16916480 | tf_op jit(solution)/shard_map/while/body/eval_jaxpr/hqk,qhd->khd/dot_general | solution.py:89
  964.1 13.3 %fusion.144 = bf16[2,16,1024]{2,1,0:T(8,128)(2,1)S(1)} fusion(bf16[1024,2,16]{0,2,1:T(8,128)(2,1)S(1)} %bitcast.215, f32[2,1024,1024]{1,2,0:T(8,128)} %fusion.142, f32[2,1024,1024]{1,2,0:T(8,128)} %get-tuple-element.366, f32[2,1024]{1,0:T(2,128)S(1)} %get-tuple-element.367), kind=kOutput, calls=%fused_computation.36.clone.1 | convolution fusion | flops 81792000 | bytes 16916480 | tf_op jit(solution)/shard_map/while/body/eval_jaxpr/hqk,khd->qhd/dot_general | solution.py:86
  984.8 6.2 fusion.143
  995.4 12.1 %fusion.145 = bf16[2,16,1024]{2,1,0:T(8,128)(2,1)S(1)} fusion(bf16[1024,2,16]{0,2,1:T(8,128)(2,1)S(1)} %bitcast.217, f32[2,1024,1024]{1,2,0:T(8,128)} %fusion.142, f32[2,1024,1024]{1,2,0:T(8,128)} %get-tuple-element.366, f32[2,1024]{1,0:T(2,128)S(1)} %get-tuple-element.367), kind=kOutput, calls=%fused_computation.35.clone.1 | convolution fusion | flops 81792000 | bytes 16916480 | tf_op jit(solution)/shard_map/while/body/eval_jaxpr/hqk,qhd->khd/dot_general | solution.py:89
  1007.5 13.3 %fusion.144 = bf16[2,16,1024]{2,1,0:T(8,128)(2,1)S(1)} fusion(bf16[1024,2,16]{0,2,1:T(8,128)(2,1)S(1)} %bitcast.215, f32[2,1024,1024]{1,2,0:T(8,128)} %fusion.142, f32[2,1024,1024]{1,2,0:T(8,128)} %get-tuple-element.366, f32[2,1024]{1,0:T(2,128)S(1)} %get-tuple-element.367), kind=kOutput, calls=%fused_computation.36.clone.1 | convolution fusion | flops 81792000 | bytes 16916480 | tf_op jit(solution)/shard_map/while/body/eval_jaxpr/hqk,khd->qhd/dot_general | solution.py:86
  1046.4 26.9 %all-to-all-done.6 = bf16[8,128,1536]{2,1,0:T(8,128)(2,1)} async-done(((bf16[8,128,1536]{2,1,0:T(8,128)(2,1)}), bf16[8,128,1536]{2,1,0:T(8,128)(2,1)}, u32[]{:S(2)}, u32[]{:S(2)}) %all-to-all-start.6) | async-done | bytes 3145760 | tf_op jit(solution)/shard_map/all_to_all | solution.py:171
  1084.9 13.4 %collective-permute-done.1 = bf16[1,512,512]{1,2,0:T(8,128)(2,1)S(1)} collective-permute-done((bf16[1,512,512]{1,2,0:T(8,128)(2,1)S(1)}, bf16[1,512,512]{1,2,0:T(8,128)(2,1)S(1)}, u32[]{:S(2)}, u32[]{:S(2)}) %collective-permute-start.1) | collective-permute-done | bytes 524320 | tf_op jit(solution)/shard_map/ppermute | solution.py:16
  (283 shorter events, 432.7 us)
Async XLA Ops:
  0.6 7.7 copy-start
  0.6 8.3 copy-start.12
  0.7 8.8 copy-start.24
  2.2 0.6 copy-start.14
  3.6 24.5 %all-to-all-start.4 = ((bf16[8,1,128]{2,1,0:T(2,128)(2,1)}), bf16[8,1,128]{2,1,0:T(2,128)(2,1)S(1)}, u32[]{:S(2)}, u32[]{:S(2)}) async-start(bf16[8,1,128]{2,1,0:T(2,128)(2,1)} %compare_convert_fusion), calls=%async_computation.4 | async-start | bytes 8192 | tf_op jit(solution)/shard_map/all_to_all | solution.py:158
  8.0 0.9 copy-start.20
  8.6 3.4 copy-start.2
  8.7 0.8 copy-start.10
  8.9 0.6 copy-start.18
  8.9 0.6 copy-start.16
  17.6 4.0 copy-start.4
  17.6 4.0 copy-start.8
  22.1 10.1 copy-start.6
  28.0 7.3 all-to-all-start.1
  35.4 18.8 %all-to-all-start.5 = ((bf16[8,128,512]{2,1,0:T(8,128)(2,1)}), bf16[8,128,512]{2,1,0:T(8,128)(2,1)S(1)}, u32[]{:S(2)}, u32[]{:S(2)}) async-start(bf16[8,128,512]{2,1,0:T(8,128)(2,1)} %select_select_fusion), calls=%async_computation.5 | async-start | bytes 2097152 | tf_op jit(solution)/shard_map/all_to_all | solution.py:160
  54.2 42.3 %all-to-all-start.3 = ((bf16[8,128,1536]{2,1,0:T(8,128)(2,1)}), bf16[8,128,1536]{2,1,0:T(8,128)(2,1)}, u32[]{:S(2)}, u32[]{:S(2)}) async-start(bf16[8,128,1536]{2,1,0:T(8,128)(2,1)} %broadcast_select_fusion.2), calls=%async_computation.3 | async-start | bytes 6291456 | tf_op jit(solution)/shard_map/all_to_all | solution.py:157
  60.1 8.3 copy-start.22
  96.5 42.3 %all-to-all-start = ((bf16[8,128,1536]{2,1,0:T(8,128)(2,1)}), bf16[8,128,1536]{2,1,0:T(8,128)(2,1)}, u32[]{:S(2)}, u32[]{:S(2)}) async-start(bf16[8,128,1536]{2,1,0:T(8,128)(2,1)} %broadcast_select_fusion.3), calls=%async_computation | async-start | bytes 6291456 | tf_op jit(solution)/shard_map/all_to_all | solution.py:153
  324.1 707.9 %all-to-all-start.2 = ((bf16[8,128,512]{2,1,0:T(8,128)(2,1)}), bf16[8,128,512]{2,1,0:T(8,128)(2,1)}, u32[]{:S(2)}, u32[]{:S(2)}) async-start(bf16[8,128,512]{2,1,0:T(8,128)(2,1)} %bitcast.26), calls=%async_computation.2 | async-start | bytes 2097152 | tf_op jit(solution)/shard_map/all_to_all | solution.py:170
  1032.0 4.8 copy-start.5
  1032.0 5.0 copy-start.15
  1032.0 5.1 copy-start.21
  1032.0 5.9 copy-start.13
  1032.0 5.9 copy-start.23
  1032.0 41.3 %all-to-all-start.6 = ((bf16[8,128,1536]{2,1,0:T(8,128)(2,1)}), bf16[8,128,1536]{2,1,0:T(8,128)(2,1)}, u32[]{:S(2)}, u32[]{:S(2)}) async-start(bf16[8,128,1536]{2,1,0:T(8,128)(2,1)} %bitcast.199), calls=%async_computation.6 | async-start | bytes 6291456 | tf_op jit(solution)/shard_map/all_to_all | solution.py:171
  1036.8 4.6 copy-start.7
  1036.8 4.6 copy-start.9
  1042.7 42.2 %collective-permute-start = (bf16[1,512,512]{2,1,0:T(8,128)(2,1)}, bf16[1,512,512]{2,1,0:T(8,128)(2,1)}, u32[]{:S(2)}, u32[]{:S(2)}) collective-permute-start(bf16[1,512,512]{2,1,0:T(8,128)(2,1)} %fusion.48), channel_id=1, source_target_pairs={{0,8},{8,16},{16,24},{1,9},{9,17},{17,25},{2,10},{10,18},{18,26},{... | collective-permute-start | bytes 1572872 | tf_op jit(solution)/shard_map/ppermute | solution.py:16
  1073.3 6.0 copy-start.3
  1073.3 6.0 copy-start.11
  1073.3 6.0 copy-start.25
  1079.3 2.5 copy-start.19
  1079.3 2.6 copy-start.17
  1081.8 19.3 %copy-start.1 = (bf16[1,4,512,512]{3,2,1,0:T(8,128)(2,1)S(1)}, bf16[1,4,512,512]{3,2,1,0:T(8,128)(2,1)}, u32[]{:S(2)}) copy-start(bf16[1,4,512,512]{3,2,1,0:T(8,128)(2,1)} %param.16) | copy-start | bytes 6291460
  1082.5 15.8 %collective-permute-start.1 = (bf16[1,512,512]{1,2,0:T(8,128)(2,1)S(1)}, bf16[1,512,512]{1,2,0:T(8,128)(2,1)S(1)}, u32[]{:S(2)}, u32[]{:S(2)}) collective-permute-start(bf16[1,512,512]{1,2,0:T(8,128)(2,1)S(1)} %fusion.64), channel_id=1, source_target_pairs={{8,0},{16,8},{24,16},{9,1},{17,9},{25,17},{10,2},{18,10},{26,18},{... | collective-permute-start | bytes 1572872 | tf_op jit(solution)/shard_map/ppermute | solution.py:16
where the time goes:
time: 1110 us; the launch traced here: 1100 us
  matrix products  823 us (74%)
  local copies, waits for them, and re-layouts  108 us (10%)
  waiting for transfers between devices  108 us (10%)
  starting transfers between devices  41.5 us (4%)
  other arithmetic  18.2 us (2%)
    dot_general x16, matrix products, one_block(): jnp.einsum('hqk,khd->qhd', score_grad, key_rows, preferred_element_type=j...  213 us
    sub x32, matrix products, block_probs(): expd = jnp.exp(score - top)  197 us
    dot_general x16, matrix products, one_block(): jnp.einsum('hqk,qhd->khd', score_grad, query, preferred_element_type=jnp....  194 us
    dot_general x16, matrix products, one_block(): jnp.einsum('hqk,qhd->khd', rounded, out_grad, preferred_element_type=jnp....  73.1 us
    dot_general x16, matrix products, one_block(): jnp.einsum('qhd,khd->hqk', out_grad, value_rows, preferred_element_type=j...  72 us
    dot_general x16, matrix products, one_block(): jnp.einsum('hqk,khd->qhd', probs, value_rows, preferred_element_type=jnp....  64.8 us
    all_to_all x1, waiting for transfers between devices, on_device(): lax.all_to_all(send_rows, 'space', split_axis=0, concat_axis=0, tiled=True)  31.3 us
    all_to_all x1, waiting for transfers between devices, on_device(): lax.all_to_all(slot_qkv, 'space', split_axis=0, concat_axis=0, tiled=True)  26.9 us
  transfers between devices with their start and end apart: 9, of which 6 were waited for; matrix products, arithmetic and copies ran while one was open for 69% of the time, Pallas kernels for 0%

commit v1 on v0

--- a/solution.py
+++ b/solution.py
@@ -168,7 +168,19 @@
     )
     slot_qkv = qkv_grads.reshape(groups, cap, 3 * width)
     ret_att = lax.all_to_all(attended, "space", split_axis=0, concat_axis=0, tiled=True)
-    ret_grads = lax.all_to_all(slot_qkv, "space", split_axis=0, concat_axis=0, tiled=True)
+    ways, here = (lax.axis_size("space"), lax.axis_index("space"))
+    width_2 = slot_qkv.shape[0] // ways
+    shape = list(slot_qkv.shape)
+    shape[0] = width_2
+    height = shape[0]
+    shape[0] = height * ways
+    full = jnp.zeros(shape, slot_qkv.dtype)
+    for mask in range(ways):
+        part = lax.dynamic_slice_in_dim(slot_qkv, (here ^ mask) * width_2, width_2, axis=0)
+        if mask:
+            part = lax.ppermute(part, "space", [(d, d ^ mask) for d in range(ways)])
+        full = lax.dynamic_update_slice_in_dim(full, part, (here ^ mask) * height, axis=0)
+    ret_grads = full
     grad_rows = jnp.take(ret_grads.reshape(slots_all, 3 * width), back_b, axis=0)
     normed_grad = jnp.dot(grad_rows, w_qkv.T, preferred_element_type=jnp.float32)
     att_rows = jnp.take(ret_att.reshape(slots_all, width), back, axis=0)

time: 1110 us -> 1060 us (0.955)
  waiting for transfers between devices: 108 us -> 64.8 us
  local copies, waits for them, and re-layouts: 108 us -> 95.3 us
    all_to_all x1, waiting for transfers between devices: 31.3 us -> 0.01 us  [on_device(): lax.all_to_all(send_rows, 'space', split_axis=0, concat_axis=0, tiled=True)]
    all_to_all x1 -> x0, waiting for transfers between devices: 26.9 us -> none  [on_device(): lax.all_to_all(slot_qkv, 'space', split_axis=0, concat_axis=0, tiled=True)]
    ppermute x0 -> x7, waiting for transfers between devices: none -> 22.6 us  [on_device(): part = lax.ppermute(part, 'space', [(d, d ^ mask) for d in range(ways)])]
  transfers between devices with their start and end apart: 9 -> 15, of which waited for: 6 -> 7; matrix products, arithmetic and copies ran while one was open for 69% -> 89% of each run, Pallas kernels for 0% -> 0%
where the time goes in v1:
time: 1060 us; the launch traced here: 1050 us
  matrix products  824 us (78%)
  local copies, waits for them, and re-layouts  95.3 us (9%)
  waiting for transfers between devices  64.8 us (6%)
  starting transfers between devices  41.5 us (4%)
  other arithmetic  21.6 us (2%)
    dot_general x16, matrix products, one_block(): jnp.einsum('hqk,khd->qhd', score_grad, key_rows, preferred_element_type=j...  213 us
    sub x32, matrix products, block_probs(): expd = jnp.exp(score - top)  197 us
    dot_general x16, matrix products, one_block(): jnp.einsum('hqk,qhd->khd', score_grad, query, preferred_element_type=jnp....  194 us
    dot_general x16, matrix products, one_block(): jnp.einsum('hqk,qhd->khd', rounded, out_grad, preferred_element_type=jnp....  73.1 us
    dot_general x16, matrix products, one_block(): jnp.einsum('qhd,khd->hqk', out_grad, value_rows, preferred_element_type=j...  72.1 us
    dot_general x16, matrix products, one_block(): jnp.einsum('hqk,khd->qhd', probs, value_rows, preferred_element_type=jnp....  64.8 us
    all_to_all x1, waiting for transfers between devices, on_device(): lax.all_to_all(send_rows_b, 'space', split_axis=0, concat_axis=0, tiled=T...  27.6 us
    ppermute x7, waiting for transfers between devices, on_device(): part = lax.ppermute(part, 'space', [(d, d ^ mask) for d in range(ways)])  22.6 us
  transfers between devices with their start and end apart: 15, of which 7 were waited for; matrix products, arithmetic and copies ran while one was open for 89% of the time, Pallas kernels for 0%

profile of v1, /device:TPU:18, one launch (start us, length us, event | category | flops | bytes accessed | tf_op | source)
XLA Modules:
  0.0 1050.2 jit_solution(11249410290221488112)
XLA Ops:
  70.9 27.6 %all-to-all-done.3 = bf16[8,128,1536]{2,1,0:T(8,128)(2,1)S(1)} async-done(((bf16[8,128,1536]{2,1,0:T(8,128)(2,1)}), bf16[8,128,1536]{2,1,0:T(8,128)(2,1)S(1)}, u32[]{:S(2)}, u32[]{:S(2)}) %all-to-all-start.3) | async-done | bytes 3145760 | tf_op jit(solution)/shard_map/all_to_all | solution.py:157
  107.6 667.9 %while.31 = (s32[]{:T(128)}, bf16[1024,1536]{0,1:T(8,128)(2,1)S(1)}, bf16[1024,1536]{0,1:T(8,128)(2,1)}, pred[1024]{0:T(1024)(128)(4,1)S(1)}, bf16[1024,512]{0,1...) while((s32[]{:T(128)}, ...), condition=%wide.region_18.20_spmd, body=%wide.region_14.19_spmd.sunk | while | flops 377494528 | bytes 60327216 | solution.py:96
  108.6 6.2 fusion.143
  119.3 12.1 %fusion.145 = bf16[2,16,1024]{2,1,0:T(8,128)(2,1)S(1)} fusion(bf16[1024,2,16]{0,2,1:T(8,128)(2,1)S(1)} %bitcast.220, f32[2,1024,1024]{1,2,0:T(8,128)} %fusion.142, f32[2,1024,1024]{1,2,0:T(8,128)} %get-tuple-element.374, f32[2,1024]{1,0:T(2,128)S(1)} %get-tuple-element.375), kind=kOutput, calls=%fused_computation.35.clone.1 | convolution fusion | flops 81792000 | bytes 16916480 | tf_op jit(solution)/shard_map/while/body/eval_jaxpr/hqk,qhd->khd/dot_general | solution.py:89
  131.4 13.3 %fusion.144 = bf16[2,16,1024]{2,1,0:T(8,128)(2,1)S(1)} fusion(bf16[1024,2,16]{0,2,1:T(8,128)(2,1)S(1)} %bitcast.218, f32[2,1024,1024]{1,2,0:T(8,128)} %fusion.142, f32[2,1024,1024]{1,2,0:T(8,128)} %get-tuple-element.374, f32[2,1024]{1,0:T(2,128)S(1)} %get-tuple-element.375), kind=kOutput, calls=%fused_computation.36.clone.1 | convolution fusion | flops 81792000 | bytes 16916480 | tf_op jit(solution)/shard_map/while/body/eval_jaxpr/hqk,khd->qhd/dot_general | solution.py:86
  150.4 6.2 fusion.143
  161.1 12.1 %fusion.145 = bf16[2,16,1024]{2,1,0:T(8,128)(2,1)S(1)} fusion(bf16[1024,2,16]{0,2,1:T(8,128)(2,1)S(1)} %bitcast.220, f32[2,1024,1024]{1,2,0:T(8,128)} %fusion.142, f32[2,1024,1024]{1,2,0:T(8,128)} %get-tuple-element.374, f32[2,1024]{1,0:T(2,128)S(1)} %get-tuple-element.375), kind=kOutput, calls=%fused_computation.35.clone.1 | convolution fusion | flops 81792000 | bytes 16916480 | tf_op jit(solution)/shard_map/while/body/eval_jaxpr/hqk,qhd->khd/dot_general | solution.py:89
  173.2 13.3 %fusion.144 = bf16[2,16,1024]{2,1,0:T(8,128)(2,1)S(1)} fusion(bf16[1024,2,16]{0,2,1:T(8,128)(2,1)S(1)} %bitcast.218, f32[2,1024,1024]{1,2,0:T(8,128)} %fusion.142, f32[2,1024,1024]{1,2,0:T(8,128)} %get-tuple-element.374, f32[2,1024]{1,0:T(2,128)S(1)} %get-tuple-element.375), kind=kOutput, calls=%fused_computation.36.clone.1 | convolution fusion | flops 81792000 | bytes 16916480 | tf_op jit(solution)/shard_map/while/body/eval_jaxpr/hqk,khd->qhd/dot_general | solution.py:86
  192.1 6.2 fusion.143
  202.8 12.1 %fusion.145 = bf16[2,16,1024]{2,1,0:T(8,128)(2,1)S(1)} fusion(bf16[1024,2,16]{0,2,1:T(8,128)(2,1)S(1)} %bitcast.220, f32[2,1024,1024]{1,2,0:T(8,128)} %fusion.142, f32[2,1024,1024]{1,2,0:T(8,128)} %get-tuple-element.374, f32[2,1024]{1,0:T(2,128)S(1)} %get-tuple-element.375), kind=kOutput, calls=%fused_computation.35.clone.1 | convolution fusion | flops 81792000 | bytes 16916480 | tf_op jit(solution)/shard_map/while/body/eval_jaxpr/hqk,qhd->khd/dot_general | solution.py:89
  214.9 13.3 %fusion.144 = bf16[2,16,1024]{2,1,0:T(8,128)(2,1)S(1)} fusion(bf16[1024,2,16]{0,2,1:T(8,128)(2,1)S(1)} %bitcast.218, f32[2,1024,1024]{1,2,0:T(8,128)} %fusion.142, f32[2,1024,1024]{1,2,0:T(8,128)} %get-tuple-element.374, f32[2,1024]{1,0:T(2,128)S(1)} %get-tuple-element.375), kind=kOutput, calls=%fused_computation.36.clone.1 | convolution fusion | flops 81792000 | bytes 16916480 | tf_op jit(solution)/shard_map/while/body/eval_jaxpr/hqk,khd->qhd/dot_general | solution.py:86
  233.9 6.2 fusion.143
  244.5 12.1 %fusion.145 = bf16[2,16,1024]{2,1,0:T(8,128)(2,1)S(1)} fusion(bf16[1024,2,16]{0,2,1:T(8,128)(2,1)S(1)} %bitcast.220, f32[2,1024,1024]{1,2,0:T(8,128)} %fusion.142, f32[2,1024,1024]{1,2,0:T(8,128)} %get-tuple-element.374, f32[2,1024]{1,0:T(2,128)S(1)} %get-tuple-element.375), kind=kOutput, calls=%fused_computation.35.clone.1 | convolution fusion | flops 81792000 | bytes 16916480 | tf_op jit(solution)/shard_map/while/body/eval_jaxpr/hqk,qhd->khd/dot_general | solution.py:89
  256.6 13.3 %fusion.144 = bf16[2,16,1024]{2,1,0:T(8,128)(2,1)S(1)} fusion(bf16[1024,2,16]{0,2,1:T(8,128)(2,1)S(1)} %bitcast.218, f32[2,1024,1024]{1,2,0:T(8,128)} %fusion.142, f32[2,1024,1024]{1,2,0:T(8,128)} %get-tuple-element.374, f32[2,1024]{1,0:T(2,128)S(1)} %get-tuple-element.375), kind=kOutput, calls=%fused_computation.36.clone.1 | convolution fusion | flops 81792000 | bytes 16916480 | tf_op jit(solution)/shard_map/while/body/eval_jaxpr/hqk,khd->qhd/dot_general | solution.py:86
  275.6 6.2 fusion.143
  286.3 12.1 %fusion.145 = bf16[2,16,1024]{2,1,0:T(8,128)(2,1)S(1)} fusion(bf16[1024,2,16]{0,2,1:T(8,128)(2,1)S(1)} %bitcast.220, f32[2,1024,1024]{1,2,0:T(8,128)} %fusion.142, f32[2,1024,1024]{1,2,0:T(8,128)} %get-tuple-element.374, f32[2,1024]{1,0:T(2,128)S(1)} %get-tuple-element.375), kind=kOutput, calls=%fused_computation.35.clone.1 | convolution fusion | flops 81792000 | bytes 16916480 | tf_op jit(solution)/shard_map/while/body/eval_jaxpr/hqk,qhd->khd/dot_general | solution.py:89
  298.4 13.3 %fusion.144 = bf16[2,16,1024]{2,1,0:T(8,128)(2,1)S(1)} fusion(bf16[1024,2,16]{0,2,1:T(8,128)(2,1)S(1)} %bitcast.218, f32[2,1024,1024]{1,2,0:T(8,128)} %fusion.142, f32[2,1024,1024]{1,2,0:T(8,128)} %get-tuple-element.374, f32[2,1024]{1,0:T(2,128)S(1)} %get-tuple-element.375), kind=kOutput, calls=%fused_computation.36.clone.1 | convolution fusion | flops 81792000 | bytes 16916480 | tf_op jit(solution)/shard_map/while/body/eval_jaxpr/hqk,khd->qhd/dot_general | solution.py:86
  317.4 6.2 fusion.143
  328.0 12.1 %fusion.145 = bf16[2,16,1024]{2,1,0:T(8,128)(2,1)S(1)} fusion(bf16[1024,2,16]{0,2,1:T(8,128)(2,1)S(1)} %bitcast.220, f32[2,1024,1024]{1,2,0:T(8,128)} %fusion.142, f32[2,1024,1024]{1,2,0:T(8,128)} %get-tuple-element.374, f32[2,1024]{1,0:T(2,128)S(1)} %get-tuple-element.375), kind=kOutput, calls=%fused_computation.35.clone.1 | convolution fusion | flops 81792000 | bytes 16916480 | tf_op jit(solution)/shard_map/while/body/eval_jaxpr/hqk,qhd->khd/dot_general | solution.py:89
  340.1 13.3 %fusion.144 = bf16[2,16,1024]{2,1,0:T(8,128)(2,1)S(1)} fusion(bf16[1024,2,16]{0,2,1:T(8,128)(2,1)S(1)} %bitcast.218, f32[2,1024,1024]{1,2,0:T(8,128)} %fusion.142, f32[2,1024,1024]{1,2,0:T(8,128)} %get-tuple-element.374, f32[2,1024]{1,0:T(2,128)S(1)} %get-tuple-element.375), kind=kOutput, calls=%fused_computation.36.clone.1 | convolution fusion | flops 81792000 | bytes 16916480 | tf_op jit(solution)/shard_map/while/body/eval_jaxpr/hqk,khd->qhd/dot_general | solution.py:86
  369.8 12.1 %fusion.145 = bf16[2,16,1024]{2,1,0:T(8,128)(2,1)S(1)} fusion(bf16[1024,2,16]{0,2,1:T(8,128)(2,1)S(1)} %bitcast.220, f32[2,1024,1024]{1,2,0:T(8,128)} %fusion.142, f32[2,1024,1024]{1,2,0:T(8,128)} %get-tuple-element.374, f32[2,1024]{1,0:T(2,128)S(1)} %get-tuple-element.375), kind=kOutput, calls=%fused_computation.35.clone.1 | convolution fusion | flops 81792000 | bytes 16916480 | tf_op jit(solution)/shard_map/while/body/eval_jaxpr/hqk,qhd->khd/dot_general | solution.py:89
  381.9 13.3 %fusion.144 = bf16[2,16,1024]{2,1,0:T(8,128)(2,1)S(1)} fusion(bf16[1024,2,16]{0,2,1:T(8,128)(2,1)S(1)} %bitcast.218, f32[2,1024,1024]{1,2,0:T(8,128)} %fusion.142, f32[2,1024,1024]{1,2,0:T(8,128)} %get-tuple-element.374, f32[2,1024]{1,0:T(2,128)S(1)} %get-tuple-element.375), kind=kOutput, calls=%fused_computation.36.clone.1 | convolution fusion | flops 81792000 | bytes 16916480 | tf_op jit(solution)/shard_map/while/body/eval_jaxpr/hqk,khd->qhd/dot_general | solution.py:86
  400.8 6.2 fusion.143
  411.5 12.1 %fusion.145 = bf16[2,16,1024]{2,1,0:T(8,128)(2,1)S(1)} fusion(bf16[1024,2,16]{0,2,1:T(8,128)(2,1)S(1)} %bitcast.220, f32[2,1024,1024]{1,2,0:T(8,128)} %fusion.142, f32[2,1024,1024]{1,2,0:T(8,128)} %get-tuple-element.374, f32[2,1024]{1,0:T(2,128)S(1)} %get-tuple-element.375), kind=kOutput, calls=%fused_computation.35.clone.1 | convolution fusion | flops 81792000 | bytes 16916480 | tf_op jit(solution)/shard_map/while/body/eval_jaxpr/hqk,qhd->khd/dot_general | solution.py:89
  423.6 13.3 %fusion.144 = bf16[2,16,1024]{2,1,0:T(8,128)(2,1)S(1)} fusion(bf16[1024,2,16]{0,2,1:T(8,128)(2,1)S(1)} %bitcast.218, f32[2,1024,1024]{1,2,0:T(8,128)} %fusion.142, f32[2,1024,1024]{1,2,0:T(8,128)} %get-tuple-element.374, f32[2,1024]{1,0:T(2,128)S(1)} %get-tuple-element.375), kind=kOutput, calls=%fused_computation.36.clone.1 | convolution fusion | flops 81792000 | bytes 16916480 | tf_op jit(solution)/shard_map/while/body/eval_jaxpr/hqk,khd->qhd/dot_general | solution.py:86
  442.6 6.2 fusion.143
  453.3 12.1 %fusion.145 = bf16[2,16,1024]{2,1,0:T(8,128)(2,1)S(1)} fusion(bf16[1024,2,16]{0,2,1:T(8,128)(2,1)S(1)} %bitcast.220, f32[2,1024,1024]{1,2,0:T(8,128)} %fusion.142, f32[2,1024,1024]{1,2,0:T(8,128)} %get-tuple-element.374, f32[2,1024]{1,0:T(2,128)S(1)} %get-tuple-element.375), kind=kOutput, calls=%fused_computation.35.clone.1 | convolution fusion | flops 81792000 | bytes 16916480 | tf_op jit(solution)/shard_map/while/body/eval_jaxpr/hqk,qhd->khd/dot_general | solution.py:89
  465.4 13.3 %fusion.144 = bf16[2,16,1024]{2,1,0:T(8,128)(2,1)S(1)} fusion(bf16[1024,2,16]{0,2,1:T(8,128)(2,1)S(1)} %bitcast.218, f32[2,1024,1024]{1,2,0:T(8,128)} %fusion.142, f32[2,1024,1024]{1,2,0:T(8,128)} %get-tuple-element.374, f32[2,1024]{1,0:T(2,128)S(1)} %get-tuple-element.375), kind=kOutput, calls=%fused_computation.36.clone.1 | convolution fusion | flops 81792000 | bytes 16916480 | tf_op jit(solution)/shard_map/while/body/eval_jaxpr/hqk,khd->qhd/dot_general | solution.py:86
  484.3 6.2 fusion.143
  495.0 12.1 %fusion.145 = bf16[2,16,1024]{2,1,0:T(8,128)(2,1)S(1)} fusion(bf16[1024,2,16]{0,2,1:T(8,128)(2,1)S(1)} %bitcast.220, f32[2,1024,1024]{1,2,0:T(8,128)} %fusion.142, f32[2,1024,1024]{1,2,0:T(8,128)} %get-tuple-element.374, f32[2,1024]{1,0:T(2,128)S(1)} %get-tuple-element.375), kind=kOutput, calls=%fused_computation.35.clone.1 | convolution fusion | flops 81792000 | bytes 16916480 | tf_op jit(solution)/shard_map/while/body/eval_jaxpr/hqk,qhd->khd/dot_general | solution.py:89
  507.1 13.3 %fusion.144 = bf16[2,16,1024]{2,1,0:T(8,128)(2,1)S(1)} fusion(bf16[1024,2,16]{0,2,1:T(8,128)(2,1)S(1)} %bitcast.218, f32[2,1024,1024]{1,2,0:T(8,128)} %fusion.142, f32[2,1024,1024]{1,2,0:T(8,128)} %get-tuple-element.374, f32[2,1024]{1,0:T(2,128)S(1)} %get-tuple-element.375), kind=kOutput, calls=%fused_computation.36.clone.1 | convolution fusion | flops 81792000 | bytes 16916480 | tf_op jit(solution)/shard_map/while/body/eval_jaxpr/hqk,khd->qhd/dot_general | solution.py:86
  526.1 6.2 fusion.143
  536.7 12.1 %fusion.145 = bf16[2,16,1024]{2,1,0:T(8,128)(2,1)S(1)} fusion(bf16[1024,2,16]{0,2,1:T(8,128)(2,1)S(1)} %bitcast.220, f32[2,1024,1024]{1,2,0:T(8,128)} %fusion.142, f32[2,1024,1024]{1,2,0:T(8,128)} %get-tuple-element.374, f32[2,1024]{1,0:T(2,128)S(1)} %get-tuple-element.375), kind=kOutput, calls=%fused_computation.35.clone.1 | convolution fusion | flops 81792000 | bytes 16916480 | tf_op jit(solution)/shard_map/while/body/eval_jaxpr/hqk,qhd->khd/dot_general | solution.py:89
  548.8 13.3 %fusion.144 = bf16[2,16,1024]{2,1,0:T(8,128)(2,1)S(1)} fusion(bf16[1024,2,16]{0,2,1:T(8,128)(2,1)S(1)} %bitcast.218, f32[2,1024,1024]{1,2,0:T(8,128)} %fusion.142, f32[2,1024,1024]{1,2,0:T(8,128)} %get-tuple-element.374, f32[2,1024]{1,0:T(2,128)S(1)} %get-tuple-element.375), kind=kOutput, calls=%fused_computation.36.clone.1 | convolution fusion | flops 81792000 | bytes 16916480 | tf_op jit(solution)/shard_map/while/body/eval_jaxpr/hqk,khd->qhd/dot_general | solution.py:86
  567.8 6.2 fusion.143
  578.5 12.1 %fusion.145 = bf16[2,16,1024]{2,1,0:T(8,128)(2,1)S(1)} fusion(bf16[1024,2,16]{0,2,1:T(8,128)(2,1)S(1)} %bitcast.220, f32[2,1024,1024]{1,2,0:T(8,128)} %fusion.142, f32[2,1024,1024]{1,2,0:T(8,128)} %get-tuple-element.374, f32[2,1024]{1,0:T(2,128)S(1)} %get-tuple-element.375), kind=kOutput, calls=%fused_computation.35.clone.1 | convolution fusion | flops 81792000 | bytes 16916480 | tf_op jit(solution)/shard_map/while/body/eval_jaxpr/hqk,qhd->khd/dot_general | solution.py:89
  590.6 13.3 %fusion.144 = bf16[2,16,1024]{2,1,0:T(8,128)(2,1)S(1)} fusion(bf16[1024,2,16]{0,2,1:T(8,128)(2,1)S(1)} %bitcast.218, f32[2,1024,1024]{1,2,0:T(8,128)} %fusion.142, f32[2,1024,1024]{1,2,0:T(8,128)} %get-tuple-element.374, f32[2,1024]{1,0:T(2,128)S(1)} %get-tuple-element.375), kind=kOutput, calls=%fused_computation.36.clone.1 | convolution fusion | flops 81792000 | bytes 16916480 | tf_op jit(solution)/shard_map/while/body/eval_jaxpr/hqk,khd->qhd/dot_general | solution.py:86
  620.2 12.1 %fusion.145 = bf16[2,16,1024]{2,1,0:T(8,128)(2,1)S(1)} fusion(bf16[1024,2,16]{0,2,1:T(8,128)(2,1)S(1)} %bitcast.220, f32[2,1024,1024]{1,2,0:T(8,128)} %fusion.142, f32[2,1024,1024]{1,2,0:T(8,128)} %get-tuple-element.374, f32[2,1024]{1,0:T(2,128)S(1)} %get-tuple-element.375), kind=kOutput, calls=%fused_computation.35.clone.1 | convolution fusion | flops 81792000 | bytes 16916480 | tf_op jit(solution)/shard_map/while/body/eval_jaxpr/hqk,qhd->khd/dot_general | solution.py:89
  632.3 13.3 %fusion.144 = bf16[2,16,1024]{2,1,0:T(8,128)(2,1)S(1)} fusion(bf16[1024,2,16]{0,2,1:T(8,128)(2,1)S(1)} %bitcast.218, f32[2,1024,1024]{1,2,0:T(8,128)} %fusion.142, f32[2,1024,1024]{1,2,0:T(8,128)} %get-tuple-element.374, f32[2,1024]{1,0:T(2,128)S(1)} %get-tuple-element.375), kind=kOutput, calls=%fused_computation.36.clone.1 | convolution fusion | flops 81792000 | bytes 16916480 | tf_op jit(solution)/shard_map/while/body/eval_jaxpr/hqk,khd->qhd/dot_general | solution.py:86
  662.0 12.1 %fusion.145 = bf16[2,16,1024]{2,1,0:T(8,128)(2,1)S(1)} fusion(bf16[1024,2,16]{0,2,1:T(8,128)(2,1)S(1)} %bitcast.220, f32[2,1024,1024]{1,2,0:T(8,128)} %fusion.142, f32[2,1024,1024]{1,2,0:T(8,128)} %get-tuple-element.374, f32[2,1024]{1,0:T(2,128)S(1)} %get-tuple-element.375), kind=kOutput, calls=%fused_computation.35.clone.1 | convolution fusion | flops 81792000 | bytes 16916480 | tf_op jit(solution)/shard_map/while/body/eval_jaxpr/hqk,qhd->khd/dot_general | solution.py:89
  674.1 13.3 %fusion.144 = bf16[2,16,1024]{2,1,0:T(8,128)(2,1)S(1)} fusion(bf16[1024,2,16]{0,2,1:T(8,128)(2,1)S(1)} %bitcast.218, f32[2,1024,1024]{1,2,0:T(8,128)} %fusion.142, f32[2,1024,1024]{1,2,0:T(8,128)} %get-tuple-element.374, f32[2,1024]{1,0:T(2,128)S(1)} %get-tuple-element.375), kind=kOutput, calls=%fused_computation.36.clone.1 | convolution fusion | flops 81792000 | bytes 16916480 | tf_op jit(solution)/shard_map/while/body/eval_jaxpr/hqk,khd->qhd/dot_general | solution.py:86
  703.7 12.1 %fusion.145 = bf16[2,16,1024]{2,1,0:T(8,128)(2,1)S(1)} fusion(bf16[1024,2,16]{0,2,1:T(8,128)(2,1)S(1)} %bitcast.220, f32[2,1024,1024]{1,2,0:T(8,128)} %fusion.142, f32[2,1024,1024]{1,2,0:T(8,128)} %get-tuple-element.374, f32[2,1024]{1,0:T(2,128)S(1)} %get-tuple-element.375), kind=kOutput, calls=%fused_computation.35.clone.1 | convolution fusion | flops 81792000 | bytes 16916480 | tf_op jit(solution)/shard_map/while/body/eval_jaxpr/hqk,qhd->khd/dot_general | solution.py:89
  715.8 13.3 %fusion.144 = bf16[2,16,1024]{2,1,0:T(8,128)(2,1)S(1)} fusion(bf16[1024,2,16]{0,2,1:T(8,128)(2,1)S(1)} %bitcast.218, f32[2,1024,1024]{1,2,0:T(8,128)} %fusion.142, f32[2,1024,1024]{1,2,0:T(8,128)} %get-tuple-element.374, f32[2,1024]{1,0:T(2,128)S(1)} %get-tuple-element.375), kind=kOutput, calls=%fused_computation.36.clone.1 | convolution fusion | flops 81792000 | bytes 16916480 | tf_op jit(solution)/shard_map/while/body/eval_jaxpr/hqk,khd->qhd/dot_general | solution.py:86
  745.5 12.1 %fusion.145 = bf16[2,16,1024]{2,1,0:T(8,128)(2,1)S(1)} fusion(bf16[1024,2,16]{0,2,1:T(8,128)(2,1)S(1)} %bitcast.220, f32[2,1024,1024]{1,2,0:T(8,128)} %fusion.142, f32[2,1024,1024]{1,2,0:T(8,128)} %get-tuple-element.374, f32[2,1024]{1,0:T(2,128)S(1)} %get-tuple-element.375), kind=kOutput, calls=%fused_computation.35.clone.1 | convolution fusion | flops 81792000 | bytes 16916480 | tf_op jit(solution)/shard_map/while/body/eval_jaxpr/hqk,qhd->khd/dot_general | solution.py:89
  757.6 13.3 %fusion.144 = bf16[2,16,1024]{2,1,0:T(8,128)(2,1)S(1)} fusion(bf16[1024,2,16]{0,2,1:T(8,128)(2,1)S(1)} %bitcast.218, f32[2,1024,1024]{1,2,0:T(8,128)} %fusion.142, f32[2,1024,1024]{1,2,0:T(8,128)} %get-tuple-element.374, f32[2,1024]{1,0:T(2,128)S(1)} %get-tuple-element.375), kind=kOutput, calls=%fused_computation.36.clone.1 | convolution fusion | flops 81792000 | bytes 16916480 | tf_op jit(solution)/shard_map/while/body/eval_jaxpr/hqk,khd->qhd/dot_general | solution.py:86
  791.4 188.2 %while.30 = (s32[]{:T(128)}, bf16[1024,512]{0,1:T(8,128)(2,1)}, bf16[1024,1536]{0,1:T(8,128)(2,1)}, pred[1024]{0:T(1024)(128)(4,1)S(1)}, s32[]{:T(128)}, /*index...) while((s32[]{:T(128)}, bf16[1024,512]{0,1:T(8,128)(2,1)}, ...), condition=%wide.region_8.10_spmd, body=%wide.region_5.9_spmd.sunk | while | flops 146801680 | bytes 17581340 | solution.py:58
  792.3 6.2 fusion.130
  804.1 6.2 fusion.130
  815.8 6.2 fusion.130
  839.4 6.2 fusion.130
  851.1 6.2 fusion.130
  862.9 6.2 fusion.130
  874.6 6.2 fusion.130
  886.4 6.2 fusion.130
  898.2 6.2 fusion.130
  909.9 6.2 fusion.130
  921.7 6.2 fusion.130
  933.5 6.2 fusion.130
  945.2 6.2 fusion.130
  957.0 6.2 fusion.130
  968.8 6.2 fusion.130
  994.1 15.2 %collective-permute-done.6 = bf16[1,128,1536]{2,1,0:T(8,128)(2,1)S(1)} collective-permute-done((bf16[1,128,1536]{2,1,0:T(8,128)(2,1)}, bf16[1,128,1536]{2,1,0:T(8,128)(2,1)S(1)}, u32[]{:S(2)}, u32[]{:S(2)}) %collective-permute-start.6) | collective-permute-done | bytes 393248 | tf_op jit(solution)/shard_map/ppermute | solution.py:181
  1009.3 7.4 collective-permute-done.7
  1042.9 6.5 collective-permute-done
  (310 shorter events, 423.3 us)
Async XLA Ops:
  0.6 7.2 copy-start
  0.6 7.8 copy-start.16
  0.7 8.9 copy-start.8
  0.7 9.4 copy-start.27
  3.0 26.9 %all-to-all-start.4 = ((bf16[8,1,128]{2,1,0:T(2,128)(2,1)}), bf16[8,1,128]{2,1,0:T(2,128)(2,1)S(1)}, u32[]{:S(2)}, u32[]{:S(2)}) async-start(bf16[8,1,128]{2,1,0:T(2,128)(2,1)} %compare_convert_fusion), calls=%async_computation.4 | async-start | bytes 8192 | tf_op jit(solution)/shard_map/all_to_all | solution.py:158
  8.1 1.9 copy-start.2
  8.2 1.8 copy-start.14
  8.4 1.6 copy-start.19
  8.4 1.6 copy-start.17
  10.0 2.7 copy-start.9
  10.1 2.7 copy-start.26
  19.4 4.0 copy-start.6
  19.4 4.0 copy-start.11
  29.9 7.3 all-to-all-start.1
  37.2 18.8 %all-to-all-start.5 = ((bf16[8,128,512]{2,1,0:T(8,128)(2,1)}), bf16[8,128,512]{2,1,0:T(8,128)(2,1)S(1)}, u32[]{:S(2)}, u32[]{:S(2)}) async-start(bf16[8,128,512]{2,1,0:T(8,128)(2,1)} %select_select_fusion), calls=%async_computation.5 | async-start | bytes 2097152 | tf_op jit(solution)/shard_map/all_to_all | solution.py:160
  56.0 1.0 copy-start.5
  57.0 41.5 %all-to-all-start.3 = ((bf16[8,128,1536]{2,1,0:T(8,128)(2,1)}), bf16[8,128,1536]{2,1,0:T(8,128)(2,1)S(1)}, u32[]{:S(2)}, u32[]{:S(2)}) async-start(bf16[8,128,1536]{2,1,0:T(8,128)(2,1)} %broadcast_select_fusion.2), calls=%async_computation.3 | async-start | bytes 6291456 | tf_op jit(solution)/shard_map/all_to_all | solution.py:157
  98.5 687.1 %all-to-all-start = ((bf16[8,128,1536]{2,1,0:T(8,128)(2,1)}), bf16[8,128,1536]{2,1,0:T(8,128)(2,1)}, u32[]{:S(2)}, u32[]{:S(2)}) async-start(bf16[8,128,1536]{2,1,0:T(8,128)(2,1)} %broadcast_select_fusion.3), calls=%async_computation | async-start | bytes 6291456 | tf_op jit(solution)/shard_map/all_to_all | solution.py:153
  778.5 1.9 copy-start.4
  781.9 204.5 %collective-permute-start.1 = (bf16[1,128,1536]{2,1,0:T(8,128)(2,1)}, bf16[1,128,1536]{2,1,0:T(8,128)(2,1)}, u32[]{:S(2)}, u32[]{:S(2)}) collective-permute-start(bf16[1,128,1536]{2,1,0:T(8,128)(2,1)} %get-tuple-element.292), channel_id=1, source_target_pairs={{0,1},{1,0},{2,3},{3,2},{4,5},{5,4},{6,7},{7,6},{8,9},{9,8},{10,11... | collective-permute-start | bytes 1179656 | tf_op jit(solution)/shard_map/ppermute | solution.py:181
  782.1 206.9 %collective-permute-start.2 = (bf16[1,128,1536]{2,1,0:T(8,128)(2,1)}, bf16[1,128,1536]{2,1,0:T(8,128)(2,1)}, u32[]{:S(2)}, u32[]{:S(2)}) collective-permute-start(bf16[1,128,1536]{2,1,0:T(8,128)(2,1)} %get-tuple-element.291), channel_id=1, source_target_pairs={{0,2},{1,3},{2,0},{3,1},{4,6},{5,7},{6,4},{7,5},{8,10},{9,11},{10,... | collective-permute-start | bytes 1179656 | tf_op jit(solution)/shard_map/ppermute | solution.py:181
  782.4 208.6 %collective-permute-start.3 = (bf16[1,128,1536]{2,1,0:T(8,128)(2,1)}, bf16[1,128,1536]{2,1,0:T(8,128)(2,1)}, u32[]{:S(2)}, u32[]{:S(2)}) collective-permute-start(bf16[1,128,1536]{2,1,0:T(8,128)(2,1)} %get-tuple-element.290), channel_id=1, source_target_pairs={{0,3},{1,2},{2,1},{3,0},{4,7},{5,6},{6,5},{7,4},{8,11},{9,10},{10,... | collective-permute-start | bytes 1179656 | tf_op jit(solution)/shard_map/ppermute | solution.py:181
  783.8 208.3 %collective-permute-start.4 = (bf16[1,128,1536]{2,1,0:T(8,128)(2,1)}, bf16[1,128,1536]{2,1,0:T(8,128)(2,1)}, u32[]{:S(2)}, u32[]{:S(2)}) collective-permute-start(bf16[1,128,1536]{2,1,0:T(8,128)(2,1)} %get-tuple-element.289), channel_id=1, source_target_pairs={{0,4},{1,5},{2,6},{3,7},{4,0},{5,1},{6,2},{7,3},{8,12},{9,13},{10,... | collective-permute-start | bytes 1179656 | tf_op jit(solution)/shard_map/ppermute | solution.py:181
  785.3 207.8 %collective-permute-start.5 = (bf16[1,128,1536]{2,1,0:T(8,128)(2,1)}, bf16[1,128,1536]{2,1,0:T(8,128)(2,1)}, u32[]{:S(2)}, u32[]{:S(2)}) collective-permute-start(bf16[1,128,1536]{2,1,0:T(8,128)(2,1)} %get-tuple-element.288), channel_id=1, source_target_pairs={{0,5},{1,4},{2,7},{3,6},{4,1},{5,0},{6,3},{7,2},{8,13},{9,12},{10,... | collective-permute-start | bytes 1179656 | tf_op jit(solution)/shard_map/ppermute | solution.py:181
  785.6 5.8 copy-start.23
  979.6 9.4 copy-start.13
  981.9 45.0 %all-to-all-start.2 = ((bf16[8,128,512]{2,1,0:T(8,128)(2,1)}), bf16[8,128,512]{2,1,0:T(8,128)(2,1)}, u32[]{:S(2)}, u32[]{:S(2)}) async-start(bf16[8,128,512]{2,1,0:T(8,128)(2,1)} %bitcast.209), calls=%async_computation.2 | async-start | bytes 2097152 | tf_op jit(solution)/shard_map/all_to_all | solution.py:170
  986.4 30.4 %copy-start.22 = (s32[1024]{0:T(1024)S(1)}, s32[1024]{0:T(1024)}, u32[]{:S(2)}) copy-start(s32[1024]{0:T(1024)} %pad_clamp_fusion) | copy-start | bytes 12292
  986.4 22.9 %collective-permute-start.6 = (bf16[1,128,1536]{2,1,0:T(8,128)(2,1)}, bf16[1,128,1536]{2,1,0:T(8,128)(2,1)S(1)}, u32[]{:S(2)}, u32[]{:S(2)}) collective-permute-start(bf16[1,128,1536]{2,1,0:T(8,128)(2,1)} %get-tuple-element.287), channel_id=1, source_target_pairs={{0,6},{1,7},{2,4},{3,5},{4,2},{5,3},{6,0},{7,1},{8,14},{9,15},{10,... | collective-permute-start | bytes 1179656 | tf_op jit(solution)/shard_map/ppermute | solution.py:181
  989.0 27.8 %collective-permute-start.7 = (bf16[1,128,1536]{2,1,0:T(8,128)(2,1)S(1)}, bf16[1,128,1536]{2,1,0:T(8,128)(2,1)S(1)}, u32[]{:S(2)}, u32[]{:S(2)}) collective-permute-start(bf16[1,128,1536]{2,1,0:T(8,128)(2,1)S(1)} %copy-done.13), channel_id=1, source_target_pairs={{0,7},{1,6},{2,5},{3,4},{4,3},{5,2},{6,1},{7,0},{8,15},{9,14},{10,... | collective-permute-start | bytes 1179656 | tf_op jit(solution)/shard_map/ppermute | solution.py:181
  1016.8 3.0 copy-start.15
  1016.8 3.0 copy-start.25
  1016.8 3.0 copy-start.28
  1019.8 3.2 copy-start.20
  1019.8 3.2 copy-start.3
  1019.8 3.2 copy-start.18
  1019.8 3.5 copy-start.7
  1023.0 3.9 copy-start.21
  1023.4 7.7 copy-start.10
  1023.4 7.7 copy-start.12
  1023.4 7.7 copy-start.24
  1024.5 16.3 %collective-permute-start.8 = (bf16[1,512,512]{1,2,0:T(8,128)(2,1)}, bf16[1,512,512]{1,2,0:T(8,128)(2,1)}, u32[]{:S(2)}, u32[]{:S(2)}) collective-permute-start(bf16[1,512,512]{1,2,0:T(8,128)(2,1)} %fusion.64), channel_id=1, source_target_pairs={{8,0},{16,8},{24,16},{9,1},{17,9},{25,17},{10,2},{18,10},{26,18},{... | collective-permute-start | bytes 1572872 | tf_op jit(solution)/shard_map/ppermute | solution.py:16
  1026.9 23.3 %copy-start.1 = (bf16[1,4,512,512]{3,2,1,0:T(8,128)(2,1)S(1)}, bf16[1,4,512,512]{3,2,1,0:T(8,128)(2,1)}, u32[]{:S(2)}) copy-start(bf16[1,4,512,512]{3,2,1,0:T(8,128)(2,1)} %param.16) | copy-start | bytes 6291460
  1033.4 15.9 %collective-permute-start = (bf16[1,512,512]{2,1,0:T(8,128)(2,1)}, bf16[1,512,512]{2,1,0:T(8,128)(2,1)S(1)}, u32[]{:S(2)}, u32[]{:S(2)}) collective-permute-start(bf16[1,512,512]{2,1,0:T(8,128)(2,1)} %fusion.48), channel_id=1, source_target_pairs={{0,8},{8,16},{16,24},{1,9},{9,17},{17,25},{2,10},{10,18},{18,26},{... | collective-permute-start | bytes 1572872 | tf_op jit(solution)/shard_map/ppermute | solution.py:16
